TPU v7x, 512 devices: a whole 4x4x16 slice. The times are simulated.
512 devices in a mesh: section: 32 (over z, core), seq: 16 (over x, y).
Axes of the slice: x: 4, y: 4, z: 16, core: 2. Of those that a mesh axis runs over, the one named last changes fastest.
Arguments:
- layer_input: bfloat16 [32, 3, 4096, 768], P('section', None, 'seq'), may hold values from -6 to 6
- grad_out: bfloat16 [32, 3, 4096, 768], P('section', None, 'seq'), may hold values from -6 to 6
- gate_weight: bfloat16 [768, 768], P('seq'), may hold values from -0.21875 to 0.21875
- mix_in_right: bfloat16 [64, 64, 64], P('seq'), may hold values from -0.75 to 0.75
- mix_in_left: bfloat16 [64, 64, 64], P('seq'), may hold values from -0.75 to 0.75
- mix_out_left: bfloat16 [64, 64, 64], P('seq'), may hold values from -0.75 to 0.75
- mix_out_right: bfloat16 [64, 64, 64], P('seq'), may hold values from -0.75 to 0.75
- kernel: bfloat16 [4096, 768], P('seq'), may hold values from -5 to 5
Outputs:
- input_grad: bfloat16 [32, 3, 4096, 768], P('section', None, 'seq')
- weight_grad: float32 [768, 768], P('seq')
- kernel_grad: bfloat16 [4096, 768], P('seq')
All inputs are finite; a program needn't handle non-finite values.
Results may differ from a plain program's by a relative error of at most 0.007.
Values may be sent and summed in bfloat16 or wider, within the bound.
A program may use at most 64 MiB of HBM per device.

v0:
```python
import math
import jax
import jax.numpy as jnp
from jax import lax
from jax.sharding import PartitionSpec as P

BATCH = 3
SEQ = 4096


def contract(form, left, right):
    return jnp.einsum(form, left, right, preferred_element_type=jnp.float32)


def forward_middle(spread, left_in, left_out, kern):
    second_mixed = contract("ija,baid->bijd", left_in, spread)
    weighted = (second_mixed * kern).astype(jnp.bfloat16)
    third_mixed = contract("ikj,bijd->bikd", left_out, weighted).astype(jnp.bfloat16)
    return (second_mixed, third_mixed)


def backward_middle(back_spread, second_mixed, left_in, left_out, kern):
    back_second = contract("ikj,bkid->bijd", left_out, back_spread)
    kernel_sum = jnp.sum(second_mixed * back_second, axis=0)
    back_weighted = (back_second * kern).astype(jnp.bfloat16)
    back_first = contract("ija,bijd->biad", left_in, back_weighted).astype(jnp.bfloat16)
    return (kernel_sum, back_first)


def local(
    layer_input,
    grad_out,
    gate_weight,
    mix_in_right,
    mix_in_left,
    mix_out_left,
    mix_out_right,
    kernel,
):
    count_batch = layer_input.shape[1]
    token_rows = layer_input.shape[2]
    width = layer_input.shape[3]
    groups = mix_in_right.shape[0]
    block_size = mix_in_right.shape[1]
    replicas = lax.axis_size("section")
    kern = kernel.reshape(groups, block_size, width).astype(jnp.float32)
    acts = layer_input[0].reshape(count_batch, groups, block_size, width)
    flat_input = layer_input[0].reshape(count_batch * token_rows, width)
    upstream = grad_out[0].reshape(count_batch * token_rows, width).astype(jnp.float32)
    weights = lax.all_gather(gate_weight, "seq", axis=0, tiled=True)
    preact = jnp.dot(flat_input, weights, preferred_element_type=jnp.float32)
    sigma = jax.nn.sigmoid(preact)
    swish = preact * sigma
    slope = sigma * (1.0 + preact * (1.0 - sigma))
    mix_grad = (
        (upstream * swish).astype(jnp.bfloat16).reshape(count_batch, groups, block_size, width)
    )
    first_mixed = contract("aic,bacd->baid", mix_in_right, acts).astype(jnp.bfloat16)
    back_third = contract("kmi,bkmd->bkid", mix_out_right, mix_grad).astype(jnp.bfloat16)
    spread = lax.all_to_all(first_mixed, "seq", split_axis=2, concat_axis=1, tiled=True)
    second_mixed, third_mixed = forward_middle(spread, mix_in_left, mix_out_left, kern)
    returned = lax.all_to_all(third_mixed, "seq", split_axis=2, concat_axis=1, tiled=True)
    back_spread = lax.all_to_all(back_third, "seq", split_axis=2, concat_axis=1, tiled=True)
    kernel_sum, back_first = backward_middle(
        back_spread, second_mixed, mix_in_left, mix_out_left, kern
    )
    back_return = lax.all_to_all(back_first, "seq", split_axis=2, concat_axis=1, tiled=True)
    mixed = contract("kmi,bikd->bkmd", mix_out_right, returned).reshape(
        count_batch * token_rows, width
    )
    gate_grad = (upstream * mixed * slope).astype(jnp.bfloat16)
    gate_part = lax.dot_general(
        gate_grad, weights, (((1,), (1,)), ((), ())), preferred_element_type=jnp.float32
    )
    weight_scale = 1.0 / math.sqrt(replicas * BATCH * SEQ)
    kernel_scale = 1.0 / math.sqrt(replicas * BATCH)
    term = lax.dot_general(
        flat_input, gate_grad, (((0,), (0,)), ((), ())), preferred_element_type=jnp.float32
    )
    weight_local = lax.psum_scatter(term * weight_scale, "seq", scatter_dimension=0, tiled=True)
    weight_grad, kernel_total = lax.psum((weight_local, kernel_sum * kernel_scale), "section")
    mix_part = contract("aic,biad->bacd", mix_in_right, back_return).reshape(
        count_batch * token_rows, width
    )
    input_grad = (
        (gate_part + mix_part).astype(jnp.bfloat16).reshape(1, count_batch, token_rows, width)
    )
    kernel_grad = kernel_total.astype(jnp.bfloat16).reshape(groups * block_size, width)
    return (input_grad, weight_grad, kernel_grad)


def solution(mesh):
    placed = (
        P("section", None, "seq", None),
        P("section", None, "seq", None),
        P("seq", None),
        P("seq", None, None),
        P("seq", None, None),
        P("seq", None, None),
        P("seq", None, None),
        P("seq", None),
    )
    return jax.shard_map(
        local,
        mesh=mesh,
        in_specs=placed,
        out_specs=(P("section", None, "seq", None), P("seq", None), P("seq", None)),
        check_vma=False,
    )
```

profile of v0, /device:TPU:2, one launch (start us, length us, event | category | flops | bytes accessed | tf_op | source)
XLA Modules:
  0.0 457.6 jit_solution(12352171297710613128)
XLA Ops:
  7.2 1.3 copy-done
  8.4 1.3 fusion.9
  9.7 1.9 copy.54
  11.7 9.5 %all-to-all-start = ((bf16[3,4,64,768]{3,1,0,2:T(4,128)(2,1)}), bf16[3,4,64,768]{3,1,0,2:T(4,128)(2,1)S(1)}, u32[]{:S(2)}, u32[]{:S(2)}) async-start(bf16[3,4,64,768]{3,1,0,2:T(4,128)(2,1)} %copy.54), calls=%async_computation | async-start | bytes 2359296 | tf_op jit(solution)/shard_map/all_to_all | solution.py:60
  22.0 0.9 convert.3
  22.9 13.2 %all-to-all-done = bf16[3,4,64,768]{3,1,0,2:T(4,128)(2,1)S(1)} async-done(((bf16[3,4,64,768]{3,1,0,2:T(4,128)(2,1)}), bf16[3,4,64,768]{3,1,0,2:T(4,128)(2,1)S(1)}, u32[]{:S(2)}, u32[]{:S(2)}) %all-to-all-start) | async-done | bytes 1179680 | tf_op jit(solution)/shard_map/all_to_all | solution.py:60
  36.6 1.2 all_to_all.55
  37.8 1.8 fusion.23
  41.1 22.2 %all_to_all.72 = bf16[3,4,64,768]{3,1,0,2:T(4,128)(2,1)S(1)} all-to-all(bf16[3,4,64,768]{3,1,0,2:T(4,128)(2,1)S(1)} %copy.56), channel_id=1, replica_groups=mesh['section'=32,'seq'=16] {'seq'}, dimensions={2} | all-to-all | bytes 2359296 | tf_op jit(solution)/shard_map/all_to_all | solution.py:62
  63.2 1.5 copy.98
  64.8 3.1 all_to_all.59
  67.9 1.8 convolution_bitcast_fusion
  69.7 1.6 copy.58
  71.2 18.5 %all-gather.2.cloned.1.call-done = bf16[768,768]{1,0:T(8,128)(2,1)} async-done(((bf16[48,768]{1,0:T(8,128)(2,1)}), bf16[768,768]{1,0:T(8,128)(2,1)}) %all-gather.2.cloned.1.call-update) | async-done | bytes 1179664 | tf_op jit(solution)/shard_map/all_gather | solution.py:50
  89.7 5.1 %fusion.1 = (bf16[768,768]{1,0:T(8,128)(2,1)S(1)}, bf16[768,768]{1,0:T(8,128)(2,1)}) fusion(f32[3,4,64,768]{3,2,1,0:T(8,128)} %copy.58, bf16[1,3,256,768]{3,2,1,0:T(8,128)(2,1)} %param.9, bf16[768,768]{1,0:T(8,128)(2,1)S(1)} %bitcast.123, bf16[768,768]{1,0:T(8,128)(2,1)} %all-gather.2.cloned.1.call-done), kind=kOutput, calls=%fused_computation.3 | convolution fusion | flops 914227200 | bytes 8257536 | tf_op jit(solution)/shard_map/dot_general | solution.py:51
  94.9 1.1 copy-done.7
  95.9 2.5 multiply_bitcast_fusion
  98.4 3.1 copy.86
  101.5 1.8 fusion.7
  104.2 22.5 %all_to_all.73 = bf16[3,4,64,768]{3,1,0,2:T(4,128)(2,1)S(1)} all-to-all(bf16[3,4,64,768]{3,1,0,2:T(4,128)(2,1)S(1)} %copy.61), channel_id=1, replica_groups=mesh['section'=32,'seq'=16] {'seq'}, dimensions={2} | all-to-all | bytes 2359296 | tf_op jit(solution)/shard_map/all_to_all | solution.py:63
  126.8 1.5 copy.97
  128.3 3.2 all_to_all.63
  131.5 2.8 fusion.5
  134.8 1.9 copy.65
  136.8 5.5 %all-to-all-start.3 = ((bf16[3,4,64,768]{3,1,0,2:T(4,128)(2,1)}), bf16[3,4,64,768]{3,1,0,2:T(4,128)(2,1)S(1)}, u32[]{:S(2)}, u32[]{:S(2)}) async-start(bf16[3,4,64,768]{3,1,0,2:T(4,128)(2,1)} %copy.65), calls=%async_computation.3 | async-start | bytes 2359296 | tf_op jit(solution)/shard_map/all_to_all | solution.py:67
  142.3 1.0 broadcast_multiply_fusion
  143.2 100.1 %all-reduce.4 = bf16[4,64,768]{2,1,0:T(8,128)(2,1)} all-reduce(f32[4,64,768]{2,1,0:T(8,128)} %broadcast_multiply_fusion), channel_id=1, replica_groups=mesh['section'=32,'seq'=16] {'section'}, use_global_device_ids=true, to_apply=%region_3.0 | all-reduce | flops 196608 | bytes 1179648 | tf_op jit(solution)/shard_map/psum | solution.py:81
  244.2 1.4 convolution_bitcast_fusion.1
  245.7 1.8 copy.87
  247.6 3.8 fusion.3
  251.3 198.0 %all-reduce.3.cloned.1.call-done = f32[48,768]{0,1:T(8,128)} async-done(((f32[48,768]{0,1:T(8,128)}), f32[48,768]{0,1:T(8,128)}) %all-reduce.3.cloned.1.call-update) | async-done | bytes 147472 | tf_op jit(solution)/shard_map/psum | solution.py:81
  449.3 1.8 copy.69
  (30 shorter events, 5.2 us)
Async XLA Ops:
  7.2 1.3 copy-start
  11.7 10.3 %copy-start.4 = (bf16[256,768]{1,0:T(8,128)(2,1)S(1)}, bf16[256,768]{1,0:T(8,128)(2,1)}, u32[]{:S(2)}) copy-start(bf16[256,768]{1,0:T(8,128)(2,1)} %param.15) | copy-start | bytes 1179652
  11.7 24.5 %all-to-all-start = ((bf16[3,4,64,768]{3,1,0,2:T(4,128)(2,1)}), bf16[3,4,64,768]{3,1,0,2:T(4,128)(2,1)S(1)}, u32[]{:S(2)}, u32[]{:S(2)}) async-start(bf16[3,4,64,768]{3,1,0,2:T(4,128)(2,1)} %copy.54), calls=%async_computation | async-start | bytes 2359296 | tf_op jit(solution)/shard_map/all_to_all | solution.py:60
  21.2 68.5 %all-gather.2.cloned.1.call-start = ((), (), s32[]{:S(2)}) async-start(), calls=%async_computation.5 | async-start | bytes 1253376 | tf_op jit(solution)/shard_map/all_gather | solution.py:50
  21.9 223.8 %reduce-scatter.4.cloned.1.call-start = ((), (), s32[]{:S(2)}) async-start(), calls=%async_computation.7 | async-start | bytes 2506752
  37.8 1.8 copy-start.1
  37.8 1.8 copy-start.5
  94.9 1.1 copy-start.7
  131.5 2.8 copy-start.2
  131.5 2.8 copy-start.6
  136.8 5.5 %copy-start.3 = (f32[4,64,768]{2,1,0:T(8,128)S(1)}, f32[4,64,768]{2,1,0:T(8,128)}, u32[]{:S(2)}) copy-start(f32[4,64,768]{2,1,0:T(8,128)} %get-tuple-element.17) | copy-start | bytes 2359300
  136.8 106.6 %all-to-all-start.3 = ((bf16[3,4,64,768]{3,1,0,2:T(4,128)(2,1)}), bf16[3,4,64,768]{3,1,0,2:T(4,128)(2,1)S(1)}, u32[]{:S(2)}, u32[]{:S(2)}) async-start(bf16[3,4,64,768]{3,1,0,2:T(4,128)(2,1)} %copy.65), calls=%async_computation.3 | async-start | bytes 2359296 | tf_op jit(solution)/shard_map/all_to_all | solution.py:67
  142.2 307.1 %all-reduce.3.cloned.1.call-start = ((), (), s32[]{:S(2)}) async-start(), calls=%async_computation.6 | async-start | bytes 786432 | tf_op jit(solution)/shard_map/psum | solution.py:81
Sparse Core Ops, SparseCore 0:
  25.1 64.5 all-gather.1
  101.6 98.0 reduce-scatter.3
  247.7 201.5 all-reduce.2
where the time goes:
time: 459 us; the launch traced here: 458 us
  waiting for transfers between devices  230 us (50%)
  blocking collectives  145 us (32%)
  local copies, waits for them, and re-layouts  28.3 us (6%)
  matrix products  23.3 us (5%)
  starting transfers between devices  15.1 us (3%)
  between operations  13.9 us (3%)
    psum x1, waiting for transfers between devices, local(): lax.psum((weight_local, kernel_sum * kernel_scale), 'section')  198 us
    psum x1, blocking collectives, local(): lax.psum((weight_local, kernel_sum * kernel_scale), 'section')  100 us
    all_to_all x1, blocking collectives, local(): lax.all_to_all(back_third, 'seq', split_axis=2, concat_axis=1, tiled=True)  22.5 us
    all_to_all x1, blocking collectives, local(): lax.all_to_all(third_mixed, 'seq', split_axis=2, concat_axis=1, tiled=True)  22.2 us
    all_gather x1, waiting for transfers between devices, local(): weights = lax.all_gather(gate_weight, 'seq', axis=0, tiled=True)  18.5 us
    all_to_all x1, waiting for transfers between devices, local(): lax.all_to_all(first_mixed, 'seq', split_axis=2, concat_axis=1, tiled=True)  13.2 us
    dot_general x8, matrix products, contract(): return jnp.einsum(form, left, right, preferred_element_type=jnp.float32)  11.8 us
    all_to_all x1, starting transfers between devices, local(): lax.all_to_all(first_mixed, 'seq', split_axis=2, concat_axis=1, tiled=True)  9.55 us
  transfers between devices with their start and end apart: 5, of which 3 were waited for; matrix products, arithmetic and copies ran while one was open for 6% of the time, Pallas kernels for 0%

commit v1 on v0

--- a/solution.py
+++ b/solution.py
@@ -47,7 +47,8 @@
     acts = layer_input[0].reshape(count_batch, groups, block_size, width)
     flat_input = layer_input[0].reshape(count_batch * token_rows, width)
     upstream = grad_out[0].reshape(count_batch * token_rows, width).astype(jnp.float32)
-    weights = lax.all_gather(gate_weight, "seq", axis=0, tiled=True)
+    stack = jnp.stack([gate_weight] * lax.axis_size("seq"))
+    weights = jnp.concatenate(lax.all_to_all(stack, "seq", 0, 0), axis=0)
     preact = jnp.dot(flat_input, weights, preferred_element_type=jnp.float32)
     sigma = jax.nn.sigmoid(preact)
     swish = preact * sigma

time: 459 us -> 454 us (0.989)
  waiting for transfers between devices: 230 us -> 214 us
  starting transfers between devices: 15.1 us -> 20.6 us
    all_gather x1 -> x0, waiting for transfers between devices: 18.5 us -> none  [local(): weights = lax.all_gather(gate_weight, 'seq', axis=0, tiled=True)]
    all_to_all x0 -> x1, starting transfers between devices: none -> 5.69 us  [local(): weights = jnp.concatenate(lax.all_to_all(stack, 'seq', 0, 0), axis=0)]
    all_to_all x0 -> x1, waiting for transfers between devices: none -> 5.45 us  [local(): weights = jnp.concatenate(lax.all_to_all(stack, 'seq', 0, 0), axis=0)]
    psum x1, blocking collectives: 100 us -> 105 us  [local(): lax.psum((weight_local, kernel_sum * kernel_scale), 'section')]
  transfers between devices with their start and end apart: 5 -> 5, of which waited for: 3 -> 3; matrix products, arithmetic and copies ran while one was open for 6% -> 5% of each run, Pallas kernels for 0% -> 0%
where the time goes in v1:
time: 454 us; the launch traced here: 453 us
  waiting for transfers between devices  214 us (47%)
  blocking collectives  148 us (33%)
  local copies, waits for them, and re-layouts  30.7 us (7%)
  matrix products  23.2 us (5%)
  starting transfers between devices  20.6 us (5%)
  between operations  14.2 us (3%)
    psum x1, waiting for transfers between devices, local(): lax.psum((weight_local, kernel_sum * kernel_scale), 'section')  194 us
    psum x1, blocking collectives, local(): lax.psum((weight_local, kernel_sum * kernel_scale), 'section')  105 us
    all_to_all x1, blocking collectives, local(): lax.all_to_all(back_third, 'seq', split_axis=2, concat_axis=1, tiled=True)  21.6 us
    all_to_all x1, blocking collectives, local(): lax.all_to_all(third_mixed, 'seq', split_axis=2, concat_axis=1, tiled=True)  21.2 us
    all_to_all x1, waiting for transfers between devices, local(): lax.all_to_all(first_mixed, 'seq', split_axis=2, concat_axis=1, tiled=True)  14 us
    dot_general x8, matrix products, contract(): return jnp.einsum(form, left, right, preferred_element_type=jnp.float32)  11.8 us
    all_to_all x1, starting transfers between devices, local(): lax.all_to_all(first_mixed, 'seq', split_axis=2, concat_axis=1, tiled=True)  9.55 us
  transfers between devices with their start and end apart: 5, of which 3 were waited for; matrix products, arithmetic and copies ran while one was open for 5% of the time, Pallas kernels for 0%

profile of v1, /device:TPU:2, one launch (start us, length us, event | category | flops | bytes accessed | tf_op | source)
XLA Modules:
  0.0 452.6 jit_solution(11425798142141487661)
XLA Ops:
  7.2 1.3 copy-done
  8.4 1.3 fusion.9
  9.7 1.9 copy.54
  11.7 9.5 %all-to-all-start = ((bf16[3,4,64,768]{3,1,0,2:T(4,128)(2,1)}), bf16[3,4,64,768]{3,1,0,2:T(4,128)(2,1)S(1)}, u32[]{:S(2)}, u32[]{:S(2)}) async-start(bf16[3,4,64,768]{3,1,0,2:T(4,128)(2,1)} %copy.54), calls=%async_computation | async-start | bytes 2359296 | tf_op jit(solution)/shard_map/all_to_all | solution.py:61
  22.1 14.0 %all-to-all-done = bf16[3,4,64,768]{3,1,0,2:T(4,128)(2,1)S(1)} async-done(((bf16[3,4,64,768]{3,1,0,2:T(4,128)(2,1)}), bf16[3,4,64,768]{3,1,0,2:T(4,128)(2,1)S(1)}, u32[]{:S(2)}, u32[]{:S(2)}) %all-to-all-start) | async-done | bytes 1179680 | tf_op jit(solution)/shard_map/all_to_all | solution.py:61
  36.6 1.2 all_to_all.58
  37.8 1.8 fusion.23
  41.1 21.2 %all_to_all.77 = bf16[3,4,64,768]{3,1,0,2:T(4,128)(2,1)} all-to-all(bf16[3,4,64,768]{3,1,0,2:T(4,128)(2,1)S(1)} %copy.56), channel_id=1, replica_groups=mesh['section'=32,'seq'=16] {'seq'}, dimensions={2} | all-to-all | bytes 2359296 | tf_op jit(solution)/shard_map/all_to_all | solution.py:63
  62.3 1.1 stack.2
  63.4 5.7 %all-to-all-start.2 = ((bf16[16,48,768]{2,1,0:T(8,128)(2,1)}), bf16[16,48,768]{2,1,0:T(8,128)(2,1)}, u32[]{:S(2)}, u32[]{:S(2)}) async-start(bf16[16,48,768]{2,1,0:T(8,128)(2,1)} %stack.2), calls=%async_computation.2 | async-start | bytes 2359296 | tf_op jit(solution)/shard_map/all_to_all | solution.py:51
  69.1 2.8 copy.98
  71.9 3.1 all_to_all.62
  75.1 1.8 convolution_bitcast_fusion
  76.8 1.6 copy.58
  78.4 5.5 %all-to-all-done.2 = bf16[16,48,768]{2,1,0:T(8,128)(2,1)} async-done(((bf16[16,48,768]{2,1,0:T(8,128)(2,1)}), bf16[16,48,768]{2,1,0:T(8,128)(2,1)}, u32[]{:S(2)}, u32[]{:S(2)}) %all-to-all-start.2) | async-done | bytes 1179680 | tf_op jit(solution)/shard_map/all_to_all | solution.py:51
  83.8 5.1 %fusion.1 = (bf16[768,768]{1,0:T(8,128)(2,1)S(1)}, bf16[768,768]{1,0:T(8,128)(2,1)}) fusion(f32[3,4,64,768]{3,2,1,0:T(8,128)} %copy.58, bf16[1,3,256,768]{3,2,1,0:T(8,128)(2,1)} %param.9, bf16[768,768]{1,0:T(8,128)(2,1)S(1)} %bitcast.124, bf16[768,768]{1,0:T(8,128)(2,1)} %bitcast.21), kind=kOutput, calls=%fused_computation.3 | convolution fusion | flops 914227200 | bytes 8257536 | tf_op jit(solution)/shard_map/dot_general | solution.py:52
  89.0 1.1 copy-done.8
  90.1 2.5 multiply_bitcast_fusion
  92.6 3.1 copy.86
  95.7 1.8 fusion.7
  98.4 21.6 %all_to_all.78 = bf16[3,4,64,768]{3,1,0,2:T(4,128)(2,1)S(1)} all-to-all(bf16[3,4,64,768]{3,1,0,2:T(4,128)(2,1)S(1)} %copy.61), channel_id=1, replica_groups=mesh['section'=32,'seq'=16] {'seq'}, dimensions={2} | all-to-all | bytes 2359296 | tf_op jit(solution)/shard_map/all_to_all | solution.py:64
  120.0 1.5 copy.97
  121.6 3.2 all_to_all.67
  124.7 2.8 fusion.5
  128.1 1.9 copy.65
  130.0 5.3 %all-to-all-start.4 = ((bf16[3,4,64,768]{3,1,0,2:T(4,128)(2,1)}), bf16[3,4,64,768]{3,1,0,2:T(4,128)(2,1)S(1)}, u32[]{:S(2)}, u32[]{:S(2)}) async-start(bf16[3,4,64,768]{3,1,0,2:T(4,128)(2,1)} %copy.65), calls=%async_computation.4 | async-start | bytes 2359296 | tf_op jit(solution)/shard_map/all_to_all | solution.py:68
  136.3 105.4 %all-reduce.4 = bf16[4,64,768]{2,1,0:T(8,128)(2,1)} all-reduce(f32[4,64,768]{2,1,0:T(8,128)} %broadcast_multiply_fusion), channel_id=1, replica_groups=mesh['section'=32,'seq'=16] {'section'}, use_global_device_ids=true, to_apply=%region_3.0 | all-reduce | flops 196608 | bytes 1179648 | tf_op jit(solution)/shard_map/psum | solution.py:82
  242.6 1.4 convolution_bitcast_fusion.1
  244.1 1.8 copy.87
  246.0 3.8 fusion.3
  249.7 194.3 %all-reduce.3.cloned.1.call-done = f32[48,768]{0,1:T(8,128)} async-done(((f32[48,768]{0,1:T(8,128)}), f32[48,768]{0,1:T(8,128)}) %all-reduce.3.cloned.1.call-update) | async-done | bytes 147472 | tf_op jit(solution)/shard_map/psum | solution.py:82
  444.0 1.8 copy.69
  (32 shorter events, 6.4 us)
Async XLA Ops:
  7.2 1.3 copy-start
  11.7 9.6 %copy-start.4 = (bf16[256,768]{1,0:T(8,128)(2,1)S(1)}, bf16[256,768]{1,0:T(8,128)(2,1)}, u32[]{:S(2)}) copy-start(bf16[256,768]{1,0:T(8,128)(2,1)} %param.15) | copy-start | bytes 1179652
  11.7 24.5 %all-to-all-start = ((bf16[3,4,64,768]{3,1,0,2:T(4,128)(2,1)}), bf16[3,4,64,768]{3,1,0,2:T(4,128)(2,1)S(1)}, u32[]{:S(2)}, u32[]{:S(2)}) async-start(bf16[3,4,64,768]{3,1,0,2:T(4,128)(2,1)} %copy.54), calls=%async_computation | async-start | bytes 2359296 | tf_op jit(solution)/shard_map/all_to_all | solution.py:61
  37.8 1.8 copy-start.1
  37.8 1.8 copy-start.5
  41.1 21.2 %copy-start.7 = (bf16[48,768]{1,0:T(8,128)(2,1)S(1)}, bf16[48,768]{1,0:T(8,128)(2,1)}, u32[]{:S(2)}) copy-start(bf16[48,768]{1,0:T(8,128)(2,1)} %param.10) | copy-start | bytes 221188
  63.4 20.4 %all-to-all-start.2 = ((bf16[16,48,768]{2,1,0:T(8,128)(2,1)}), bf16[16,48,768]{2,1,0:T(8,128)(2,1)}, u32[]{:S(2)}, u32[]{:S(2)}) async-start(bf16[16,48,768]{2,1,0:T(8,128)(2,1)} %stack.2), calls=%async_computation.2 | async-start | bytes 2359296 | tf_op jit(solution)/shard_map/all_to_all | solution.py:51
  69.1 175.0 %reduce-scatter.4.cloned.1.call-start = ((), (), s32[]{:S(2)}) async-start(), calls=%async_computation.7 | async-start | bytes 2506752
  89.0 1.1 copy-start.8
  124.7 2.8 copy-start.2
  124.7 2.8 copy-start.6
  130.0 5.3 %copy-start.3 = (f32[4,64,768]{2,1,0:T(8,128)S(1)}, f32[4,64,768]{2,1,0:T(8,128)}, u32[]{:S(2)}) copy-start(f32[4,64,768]{2,1,0:T(8,128)} %get-tuple-element.17) | copy-start | bytes 2359300
  130.0 111.7 %all-to-all-start.4 = ((bf16[3,4,64,768]{3,1,0,2:T(4,128)(2,1)}), bf16[3,4,64,768]{3,1,0,2:T(4,128)(2,1)S(1)}, u32[]{:S(2)}, u32[]{:S(2)}) async-start(bf16[3,4,64,768]{3,1,0,2:T(4,128)(2,1)} %copy.65), calls=%async_computation.4 | async-start | bytes 2359296 | tf_op jit(solution)/shard_map/all_to_all | solution.py:68
  135.3 308.7 %all-reduce.3.cloned.1.call-start = ((), (), s32[]{:S(2)}) async-start(), calls=%async_computation.6 | async-start | bytes 786432 | tf_op jit(solution)/shard_map/psum | solution.py:82
Sparse Core Ops, SparseCore 0:
  95.8 99.1 reduce-scatter.3
  246.1 197.8 all-reduce.2
